TPU v7x, 256 devices: a whole 4x4x8 slice. The times are simulated.
256 devices in a mesh: rep: 16 (over y_lo, z), tp: 16 (over x, y_hi, core).
Axes of the slice: x: 4, y: 4 (y_hi: 2, y_lo: 2; y = y_hi * 2 + y_lo), z: 8, core: 2. Of those that a mesh axis runs over, the one named last changes fastest.
Arguments:
- tokens: bfloat16 [16384, 8192], P('rep', 'tp'), may hold values from -6 to 6
- grad_out: bfloat16 [16384, 4096], P('rep', 'tp'), may hold values from -0.046875 to 0.046875
- lengths: int32 [16, 16], replicated, may hold values from 0 to 256, as said below
- master: float32 [8192, 2048], P('rep', 'tp'), may hold values from -3 to 3
- first: float32 [8192, 2048], P('rep', 'tp'), may hold values from -6 to 6
- second: float32 [8192, 2048], P('rep', 'tp'), may hold values from 0.25 to 4
Outputs:
- new_master: float32 [8192, 2048], P('rep', 'tp')
- new_first: float32 [8192, 2048], P('rep', 'tp')
- new_second: float32 [8192, 2048], P('rep', 'tp')
- healthy_weights: bfloat16 [8192, 2048], P(None, 'tp')
- slot_weights: bfloat16 [16, 8192, 4096], P('rep', None, 'tp')
Inputs may be any that keep to these rules, and one draw needn't show every extreme that they name: `lengths`: each row is one replica's split of the 2048 columns over its devices in tp order: the entries are multiples of 64, sum to 2048, the nonzero ones come first and number at least half of the row; a row is either all 128 or has an entry equal to 256, and some row has an entry equal to 256.
All inputs are finite; a program needn't handle non-finite values.
Results may differ from a plain program's by a relative error of at most 0.0019.
Values may be sent and summed in bfloat16 or wider, within the bound.
No kernel may reach another device: no remote copies, remote signals or barrier semaphores. Data moves between devices by JAX's collectives and lax.ppermute only.
A program may use at most 128 MiB of HBM per device.

v0:
```python
import jax
import jax.numpy as jnp
from jax import lax
from jax.sharding import Mesh
from jax.sharding import PartitionSpec as P

COLS = 2048
STEP = 1000
REP = ("rep_0", "rep_1")
decay_first = 0.9
decay_second = 0.999
learning_rate = 0.02
weight_decay = 0.1
epsilon = 1e-08


def own_block(parts, axes, turns):
    inside = parts.shape[1:]
    parts = parts.reshape(*(lax.axis_size(a) for a in axes), *inside)
    parts = jnp.moveaxis(parts, turns, range(len(axes))).reshape(-1, *inside)
    for k in turns:
        parts = lax.psum_scatter(parts, axes[k], scatter_dimension=0, tiled=True)
    return parts[0]


def in_blocks(value, dim, size):
    before, after = (value.shape[:dim], value.shape[dim + 1 :])
    return jnp.moveaxis(value.reshape(*before, size, -1, *after), dim, 0)


def summed_rows(value, axes, turns, dim):
    size = lax.axis_size(axes)
    return own_block(in_blocks(value, dim, size), axes, turns)


def from_everyone(value, axis):
    copies = jnp.broadcast_to(value, (lax.axis_size(axis), *value.shape))
    return lax.all_to_all(copies, axis, split_axis=0, concat_axis=0, tiled=True)


def laid_out(parts, dim):
    shape = list(parts.shape[1:])
    shape[dim] *= parts.shape[0]
    return jnp.moveaxis(parts, 0, dim).reshape(shape)


def gathered_copies(value, axis, dim):
    parts = from_everyone(value, axis)
    return laid_out(parts, dim)


def adam_update(master, first, second, gradient):
    scale_first = 1.0 - decay_first**STEP
    scale_second = 1.0 - decay_second**STEP
    new_first = decay_first * first + (1.0 - decay_first) * gradient
    new_second = decay_second * second + (1.0 - decay_second) * gradient * gradient
    direction = new_first / scale_first / (jnp.sqrt(new_second / scale_second) + epsilon)
    new_master = master - learning_rate * (direction + weight_decay * master)
    return (new_master, new_first, new_second)


def on_device(tokens, grad_out, lengths, master, first, second):
    shards = lax.axis_size("tp")
    replicas = lax.axis_size(REP)
    column_index = lax.axis_index("tp")
    replica_index = lax.axis_index(REP)
    token_count = tokens.shape[0]
    slot_width = grad_out.shape[1]
    block_width = COLS // shards
    begins_all = jnp.cumsum(lengths, axis=1) - lengths
    is_mine = jnp.arange(shards, dtype=jnp.int32) == column_index
    own_lengths = lax.dynamic_index_in_dim(lengths, replica_index, 0, keepdims=False)
    own_begins = lax.dynamic_index_in_dim(begins_all, replica_index, 0, keepdims=False)
    my_begin = jnp.sum(jnp.where(is_mine, own_begins, 0))
    my_length = jnp.sum(jnp.where(is_mine, own_lengths, 0))
    columns = jnp.arange(COLS, dtype=jnp.int32)
    offset = columns - my_begin
    inside = (offset >= 0) & (offset < my_length)
    picked = jnp.take(grad_out, jnp.clip(offset, 0, slot_width - 1), axis=1)
    spread = jnp.where(inside[None, :], picked, jnp.zeros_like(picked)).reshape(
        token_count, shards, block_width
    )
    received = lax.all_to_all(spread, "tp", split_axis=1, concat_axis=1, tiled=True)
    grad_block = jnp.sum(received, axis=1)
    grad_columns = lax.dot_general(
        lax.all_gather(tokens, "tp", axis=1, tiled=True),
        grad_block,
        (((0,), (0,)), ((), ())),
        preferred_element_type=jnp.float32,
    )
    summed = summed_rows(grad_columns.astype(jnp.bfloat16), REP, (1, 0), 0).astype(jnp.float32)
    new_master, new_first, new_second = adam_update(master, first, second, summed)
    weights = new_master.astype(jnp.bfloat16)
    healthy = gathered_copies(weights, REP, 0)
    replica_rows = lax.all_gather(weights, "tp", axis=1, tiled=True)
    slot_begins = jnp.sum(jnp.where(is_mine[None, :], begins_all, 0), axis=1)
    slot_lengths = jnp.sum(jnp.where(is_mine[None, :], lengths, 0), axis=1)
    within = jnp.arange(slot_width, dtype=jnp.int32)
    source_cols = slot_begins[:, None] + within[None, :]
    valid = within[None, :] < slot_lengths[:, None]
    taken = jnp.take(replica_rows, jnp.clip(source_cols, 0, COLS - 1).reshape(-1), axis=1)
    outgoing = jnp.where(valid.reshape(-1)[None, :], taken, jnp.zeros_like(taken))
    outgoing = outgoing.reshape(replica_rows.shape[0], replicas, slot_width)
    arrived = lax.all_to_all(outgoing, REP, split_axis=1, concat_axis=0, tiled=True)
    slot_weights = arrived.reshape(1, -1, slot_width)
    return (new_master, new_first, new_second, healthy, slot_weights)


def solution(mesh):
    torus = Mesh(mesh.devices.reshape(2, 8, mesh.shape["tp"]), ("rep_0", "rep_1", "tp"))
    placed = (P(REP, "tp"), P(REP, "tp"), P(), P(REP, "tp"), P(REP, "tp"), P(REP, "tp"))
    return jax.shard_map(
        on_device,
        mesh=torus,
        in_specs=placed,
        out_specs=(P(REP, "tp"), P(REP, "tp"), P(REP, "tp"), P(None, "tp"), P(REP, None, "tp")),
        check_vma=False,
    )
```

profile of v0, /device:TPU:32, one launch (start us, length us, event | category | flops | bytes accessed | tf_op | source)
XLA Modules:
  0.0 450.8 jit_solution(10688095374911271748)
XLA Ops:
  8.0 0.9 reduce_window_sum.11
  8.8 1.2 copy.34
  10.9 1.3 fusion.12
  12.9 9.6 %gather_fusion = bf16[2048,1024]{1,0:T(8,128)(2,1)} fusion(bf16[1024,256]{0,1:T(8,128)(2,1)S(1)} %copy.34, s32[2048]{0:T(1024)S(1)} %broadcast_clamp_fusion.1), kind=kCustom, calls=%fused_computation | custom fusion | bytes 8396800 | tf_op jit(solution)/shard_map/jit(_take)/gather | solution.py:79
  23.2 1.3 fusion.11
  24.5 3.1 select_select_fusion.1
  27.6 73.9 %all_to_all.25 = bf16[1024,16,128]{0,2,1:T(8,128)(2,1)} all-to-all(bf16[1024,16,128]{0,2,1:T(8,128)(2,1)S(1)} %select_select_fusion.1), channel_id=1, replica_groups=mesh['rep_0'=2,'rep_1'=8,'tp'=16] {'tp'}, dimensions={1} | all-to-all | bytes 8388608 | tf_op jit(solution)/shard_map/all_to_all | solution.py:83
  101.5 3.1 reduce_sum.50
  104.7 63.9 %all-gather.3.cloned.1.call-done = bf16[1024,8192]{1,0:T(8,128)(2,1)} async-done(((bf16[1024,512]{1,0:T(8,128)(2,1)}), bf16[1024,8192]{1,0:T(8,128)(2,1)}) %all-gather.3.cloned.1.call-update) | async-done | bytes 16777232 | tf_op jit(solution)/shard_map/all_gather | solution.py:86
  168.6 8.1 %convolution_convert_fusion = bf16[128,8192]{1,0:T(8,128)(2,1)S(1)} fusion(bf16[1024,128]{0,1:T(8,128)(2,1)S(1)} %reduce_sum.50, bf16[1024,8192]{1,0:T(8,128)(2,1)} %all-gather.3.cloned.1.call-done), kind=kOutput, calls=%fused_computation.2 | convolution fusion | flops 2148532224 | bytes 19136512 | tf_op jit(solution)/shard_map/dot_general | solution.py:85
  177.6 2.5 copy.35
  180.2 41.0 %reduce-scatter.3.cloned.1.call-done = bf16[2,512,128]{1,2,0:T(8,128)(2,1)} async-done(((bf16[16,512,128]{1,2,0:T(8,128)(2,1)}), bf16[2,512,128]{1,2,0:T(8,128)(2,1)}) %reduce-scatter.3.cloned.1.call-update) | async-done | bytes 262160 | tf_op jit(solution)/shard_map/reduce_scatter | solution.py:22
  221.7 18.0 %reduce-scatter.5.cloned.1.call-done = bf16[1,512,128]{1,2,0:T(8,128)(2,1)} async-done(((bf16[2,512,128]{1,2,0:T(8,128)(2,1)}), bf16[1,512,128]{1,2,0:T(8,128)(2,1)}) %reduce-scatter.5.cloned.1.call-update) | async-done | bytes 131088 | tf_op jit(solution)/shard_map/reduce_scatter | solution.py:22
  239.7 1.8 fusion.14
  241.5 1.0 copy.39
  242.5 1.7 broadcast_in_dim.78
  244.3 7.5 %all-to-all-start.1 = ((bf16[16,512,128]{2,1,0:T(8,128)(2,1)}), bf16[16,512,128]{2,1,0:T(8,128)(2,1)S(1)}, u32[]{:S(2)}, u32[]{:S(2)}) async-start(bf16[16,512,128]{2,1,0:T(8,128)(2,1)} %broadcast_in_dim.78), calls=%async_computation.3 | async-start | bytes 4194304 | tf_op jit(solution)/shard_map/all_to_all | solution.py:38
  252.0 52.9 %all-gather.5.cloned.1.call-done = bf16[512,2048]{0,1:T(8,128)(2,1)} async-done(((bf16[512,128]{0,1:T(8,128)(2,1)}), bf16[512,2048]{0,1:T(8,128)(2,1)}) %all-gather.5.cloned.1.call-update) | async-done | bytes 2097168 | tf_op jit(solution)/shard_map/all_gather | solution.py:95
  304.9 19.3 %gather_fusion.1 = bf16[4096,512]{1,0:T(8,128)(2,1)} fusion(bf16[512,2048]{0,1:T(8,128)(2,1)} %all-gather.5.cloned.1.call-done, s32[4096]{0:T(1024)S(1)} %broadcast_clamp_fusion), kind=kCustom, calls=%fused_computation.1 | custom fusion | bytes 8404992 | tf_op jit(solution)/shard_map/jit(_take)/gather | solution.py:101
  324.2 5.2 %select_select_fusion = bf16[512,16,256]{0,2,1:T(8,128)(2,1)} fusion(bf16[512,16,256]{0,2,1:T(8,128)(2,1)} %bitcast.43, pred[16,256]{1,0:T(8,128)(4,1)S(1)} %get-tuple-element.30, pred[16,256]{1,0:T(8,128)(4,1)S(1)} %get-tuple-element.29), kind=kLoop, calls=%fused_computation.3 | loop fusion | flops 4194304 | bytes 8396800 | tf_op jit(solution)/shard_map/jit(_where)/select_n | solution.py:102
  329.5 11.3 %all-to-all-start.2 = ((bf16[512,16,256]{0,2,1:T(8,128)(2,1)}), bf16[512,16,256]{0,2,1:T(8,128)(2,1)}, u32[]{:S(2)}, u32[]{:S(2)}) async-start(bf16[512,16,256]{0,2,1:T(8,128)(2,1)} %select_select_fusion), calls=%async_computation.4 | async-start | bytes 8388608 | tf_op jit(solution)/shard_map/all_to_all | solution.py:104
  343.2 93.3 %all-to-all-done.2 = bf16[512,16,256]{0,2,1:T(8,128)(2,1)} async-done(((bf16[512,16,256]{0,2,1:T(8,128)(2,1)}), bf16[512,16,256]{0,2,1:T(8,128)(2,1)}, u32[]{:S(2)}, u32[]{:S(2)}) %all-to-all-start.2) | async-done | bytes 4194336 | tf_op jit(solution)/shard_map/all_to_all | solution.py:104
  436.6 6.4 %copy.40 = bf16[16,512,1,256]{3,1,0,2:T(8,128)(2,1)} copy(bf16[16,512,1,256]{1,3,0,2:T(8,128)(2,1)} %bitcast.15) | data formatting | bytes 8388608 | tf_op jit(solution)/shard_map/all_to_all | solution.py:104
  443.0 1.3 copy.47
  (32 shorter events, 7.0 us)
Async XLA Ops:
  7.2 161.4 %all-gather.3.cloned.1.call-start = ((), (), s32[]{:S(2)}) async-start(), calls=%async_computation.5 | async-start | bytes 17825792 | tf_op jit(solution)/shard_map/all_gather | solution.py:86
  7.9 213.3 %reduce-scatter.3.cloned.1.call-start = ((), (), s32[]{:S(2)}) async-start(), calls=%async_computation.6 | async-start | bytes 2359296 | tf_op jit(solution)/shard_map/reduce_scatter | solution.py:22
  177.6 43.7 %copy-start = (f32[512,128]{1,0:T(8,128)S(1)}, f32[512,128]{1,0:T(8,128)}, u32[]{:S(2)}) copy-start(f32[512,128]{1,0:T(8,128)} %param.10) | copy-start | bytes 786436
  177.6 43.8 %copy-start.1 = (f32[512,128]{1,0:T(8,128)S(1)}, f32[512,128]{1,0:T(8,128)}, u32[]{:S(2)}) copy-start(f32[512,128]{1,0:T(8,128)} %param.11) | copy-start | bytes 786436
  177.6 43.9 %copy-start.2 = (f32[512,128]{1,0:T(8,128)S(1)}, f32[512,128]{1,0:T(8,128)}, u32[]{:S(2)}) copy-start(f32[512,128]{1,0:T(8,128)} %param.9) | copy-start | bytes 786436
  180.1 59.6 %reduce-scatter.5.cloned.1.call-start = ((), (), s32[]{:S(2)}) async-start(), calls=%async_computation.7 | async-start | bytes 393216 | tf_op jit(solution)/shard_map/reduce_scatter | solution.py:22
  221.2 83.7 %all-gather.5.cloned.1.call-start = ((), (), s32[]{:S(2)}) async-start(), calls=%async_computation.8 | async-start | bytes 2228224 | tf_op jit(solution)/shard_map/all_gather | solution.py:95
  244.3 85.2 %all-to-all-start.1 = ((bf16[16,512,128]{2,1,0:T(8,128)(2,1)}), bf16[16,512,128]{2,1,0:T(8,128)(2,1)S(1)}, u32[]{:S(2)}, u32[]{:S(2)}) async-start(bf16[16,512,128]{2,1,0:T(8,128)(2,1)} %broadcast_in_dim.78), calls=%async_computation.3 | async-start | bytes 4194304 | tf_op jit(solution)/shard_map/all_to_all | solution.py:38
  329.5 107.1 %all-to-all-start.2 = ((bf16[512,16,256]{0,2,1:T(8,128)(2,1)}), bf16[512,16,256]{0,2,1:T(8,128)(2,1)}, u32[]{:S(2)}, u32[]{:S(2)}) async-start(bf16[512,16,256]{0,2,1:T(8,128)(2,1)} %select_select_fusion), calls=%async_computation.4 | async-start | bytes 8388608 | tf_op jit(solution)/shard_map/all_to_all | solution.py:104
Sparse Core Ops, SparseCore 0:
  10.5 158.0 all-gather.2
  180.3 40.8 reduce-scatter.2
  223.7 16.0 reduce-scatter.4
  242.8 62.0 all-gather.4
where the time goes:
time: 452 us; the launch traced here: 451 us
  waiting for transfers between devices  270 us (60%)
  blocking collectives  73.9 us (16%)
  local copies, waits for them, and re-layouts  46.9 us (10%)
  other arithmetic  19.1 us (4%)
  starting transfers between devices  18.9 us (4%)
  between operations  13.9 us (3%)
  matrix products  8.12 us (2%)
    all_to_all x1, waiting for transfers between devices, on_device(): lax.all_to_all(outgoing, REP, split_axis=1, concat_axis=0, tiled=True)  93.3 us
    all_to_all x1, blocking collectives, on_device(): lax.all_to_all(spread, 'tp', split_axis=1, concat_axis=1, tiled=True)  73.9 us
    all_gather x1, waiting for transfers between devices, on_device(): lax.all_gather(tokens, 'tp', axis=1, tiled=True)  63.9 us
    reduce_scatter x2, waiting for transfers between devices, own_block(): parts = lax.psum_scatter(parts, axes[k], scatter_dimension=0, tiled=True)  59 us
    all_gather x1, waiting for transfers between devices, on_device(): replica_rows = lax.all_gather(weights, 'tp', axis=1, tiled=True)  52.9 us
    gather x1, local copies, waits for them, and re-layouts, on_device(): jnp.take(replica_rows, jnp.clip(source_cols, 0, COLS - 1).reshape(-1), ax...  19.3 us
    all_to_all x1, starting transfers between devices, on_device(): lax.all_to_all(outgoing, REP, split_axis=1, concat_axis=0, tiled=True)  11.3 us
    gather x1, local copies, waits for them, and re-layouts, on_device(): picked = jnp.take(grad_out, jnp.clip(offset, 0, slot_width - 1), axis=1)  9.61 us
  transfers between devices with their start and end apart: 6, of which 5 were waited for; matrix products, arithmetic and copies ran while one was open for 12% of the time, Pallas kernels for 0%

commit v1 on v0

--- a/solution.py
+++ b/solution.py
@@ -101,7 +101,11 @@
     taken = jnp.take(replica_rows, jnp.clip(source_cols, 0, COLS - 1).reshape(-1), axis=1)
     outgoing = jnp.where(valid.reshape(-1)[None, :], taken, jnp.zeros_like(taken))
     outgoing = outgoing.reshape(replica_rows.shape[0], replicas, slot_width)
-    arrived = lax.all_to_all(outgoing, REP, split_axis=1, concat_axis=0, tiled=True)
+    base_arr = lax.axis_size(REP)
+    all_rows = jnp.split(outgoing, base_arr, axis=1)
+    x_new = jnp.stack(all_rows)
+    left_arr = lax.all_to_all(x_new, REP, 0, 0)
+    arrived = jnp.concatenate(left_arr, axis=0)
     slot_weights = arrived.reshape(1, -1, slot_width)
     return (new_master, new_first, new_second, healthy, slot_weights)
 

time: 452 us -> 462 us (1.022)
  local copies, waits for them, and re-layouts: 46.9 us -> 58.4 us
    unnamed x16 -> x31, local copies, waits for them, and re-layouts: 6.35 us -> 17.1 us
  transfers between devices with their start and end apart: 6 -> 6, of which waited for: 5 -> 5; matrix products, arithmetic and copies ran while one was open for 12% -> 14% of each run, Pallas kernels for 0% -> 0%
where the time goes in v1:
time: 462 us; the launch traced here: 461 us
  waiting for transfers between devices  270 us (58%)
  blocking collectives  73.9 us (16%)
  local copies, waits for them, and re-layouts  58.4 us (13%)
  starting transfers between devices  18.9 us (4%)
  other arithmetic  17.5 us (4%)
  between operations  14 us (3%)
  matrix products  8.12 us (2%)
    all_to_all x1, waiting for transfers between devices, on_device(): left_arr = lax.all_to_all(x_new, REP, 0, 0)  93.3 us
    all_to_all x1, blocking collectives, on_device(): lax.all_to_all(spread, 'tp', split_axis=1, concat_axis=1, tiled=True)  73.9 us
    all_gather x1, waiting for transfers between devices, on_device(): lax.all_gather(tokens, 'tp', axis=1, tiled=True)  63.9 us
    reduce_scatter x2, waiting for transfers between devices, own_block(): parts = lax.psum_scatter(parts, axes[k], scatter_dimension=0, tiled=True)  59 us
    all_gather x1, waiting for transfers between devices, on_device(): replica_rows = lax.all_gather(weights, 'tp', axis=1, tiled=True)  53.1 us
    gather x1, local copies, waits for them, and re-layouts, on_device(): jnp.take(replica_rows, jnp.clip(source_cols, 0, COLS - 1).reshape(-1), ax...  19.3 us
    unnamed x31, local copies, waits for them, and re-layouts  17.1 us
    all_to_all x1, starting transfers between devices, on_device(): left_arr = lax.all_to_all(x_new, REP, 0, 0)  11.3 us
  transfers between devices with their start and end apart: 6, of which 5 were waited for; matrix products, arithmetic and copies ran while one was open for 14% of the time, Pallas kernels for 0%

profile of v1, /device:TPU:32, one launch (start us, length us, event | category | flops | bytes accessed | tf_op | source)
XLA Modules:
  0.0 460.9 jit_solution(7702166508178307617)
XLA Ops:
  8.0 0.9 reduce_window_sum.11
  8.8 1.2 copy.34
  10.9 1.3 fusion.28
  12.9 9.6 %gather_fusion = bf16[2048,1024]{1,0:T(8,128)(2,1)} fusion(bf16[1024,256]{0,1:T(8,128)(2,1)S(1)} %copy.34, s32[2048]{0:T(1024)S(1)} %broadcast_clamp_fusion.1), kind=kCustom, calls=%fused_computation | custom fusion | bytes 8396800 | tf_op jit(solution)/shard_map/jit(_take)/gather | solution.py:79
  23.2 1.3 fusion.27
  24.5 3.1 select_select_fusion.1
  27.6 73.9 %all_to_all.15 = bf16[1024,16,128]{0,2,1:T(8,128)(2,1)} all-to-all(bf16[1024,16,128]{0,2,1:T(8,128)(2,1)S(1)} %select_select_fusion.1), channel_id=1, replica_groups=mesh['rep_0'=2,'rep_1'=8,'tp'=16] {'tp'}, dimensions={1} | all-to-all | bytes 8388608 | tf_op jit(solution)/shard_map/all_to_all | solution.py:83
  101.5 3.1 reduce_sum.50
  104.7 63.9 %all-gather.3.cloned.1.call-done = bf16[1024,8192]{1,0:T(8,128)(2,1)} async-done(((bf16[1024,512]{1,0:T(8,128)(2,1)}), bf16[1024,8192]{1,0:T(8,128)(2,1)}) %all-gather.3.cloned.1.call-update) | async-done | bytes 16777232 | tf_op jit(solution)/shard_map/all_gather | solution.py:86
  168.6 8.1 %convolution_convert_fusion = bf16[128,8192]{1,0:T(8,128)(2,1)S(1)} fusion(bf16[1024,128]{0,1:T(8,128)(2,1)S(1)} %reduce_sum.50, bf16[1024,8192]{1,0:T(8,128)(2,1)} %all-gather.3.cloned.1.call-done), kind=kOutput, calls=%fused_computation.2 | convolution fusion | flops 2148532224 | bytes 19136512 | tf_op jit(solution)/shard_map/dot_general | solution.py:85
  177.6 2.5 copy.35
  180.2 41.0 %reduce-scatter.3.cloned.1.call-done = bf16[2,512,128]{1,2,0:T(8,128)(2,1)} async-done(((bf16[16,512,128]{1,2,0:T(8,128)(2,1)}), bf16[2,512,128]{1,2,0:T(8,128)(2,1)}) %reduce-scatter.3.cloned.1.call-update) | async-done | bytes 262160 | tf_op jit(solution)/shard_map/reduce_scatter | solution.py:22
  221.7 18.0 %reduce-scatter.5.cloned.1.call-done = bf16[1,512,128]{1,2,0:T(8,128)(2,1)} async-done(((bf16[2,512,128]{1,2,0:T(8,128)(2,1)}), bf16[1,512,128]{1,2,0:T(8,128)(2,1)}) %reduce-scatter.5.cloned.1.call-update) | async-done | bytes 131088 | tf_op jit(solution)/shard_map/reduce_scatter | solution.py:22
  239.7 1.8 fusion.30
  241.7 1.0 copy.39
  242.8 1.7 broadcast_in_dim.78
  244.5 7.5 %all-to-all-start.1 = ((bf16[16,512,128]{2,1,0:T(8,128)(2,1)}), bf16[16,512,128]{2,1,0:T(8,128)(2,1)S(1)}, u32[]{:S(2)}, u32[]{:S(2)}) async-start(bf16[16,512,128]{2,1,0:T(8,128)(2,1)} %broadcast_in_dim.78), calls=%async_computation.3 | async-start | bytes 4194304 | tf_op jit(solution)/shard_map/all_to_all | solution.py:38
  252.0 53.1 %all-gather.5.cloned.1.call-done = bf16[512,2048]{0,1:T(8,128)(2,1)} async-done(((bf16[512,128]{0,1:T(8,128)(2,1)}), bf16[512,2048]{0,1:T(8,128)(2,1)}) %all-gather.5.cloned.1.call-update) | async-done | bytes 2097168 | tf_op jit(solution)/shard_map/all_gather | solution.py:95
  305.2 19.3 %gather_fusion.1 = bf16[4096,512]{1,0:T(8,128)(2,1)} fusion(bf16[512,2048]{0,1:T(8,128)(2,1)} %all-gather.5.cloned.1.call-done, s32[4096]{0:T(1024)S(1)} %broadcast_clamp_fusion), kind=kCustom, calls=%fused_computation.1 | custom fusion | bytes 8404992 | tf_op jit(solution)/shard_map/jit(_take)/gather | solution.py:101
  324.5 3.6 select_select_fusion
  339.6 11.3 %all-to-all-start.2 = ((bf16[16,512,1,256]{1,3,2,0:T(8,128)(2,1)}), bf16[16,512,1,256]{1,3,2,0:T(8,128)(2,1)}, u32[]{:S(2)}, u32[]{:S(2)}) async-start(bf16[16,512,1,256]{1,3,2,0:T(8,128)(2,1)} %fusion.2), calls=%async_computation.4 | async-start | bytes 8388608 | tf_op jit(solution)/shard_map/all_to_all | solution.py:107
  353.4 93.3 %all-to-all-done.2 = bf16[16,512,1,256]{1,3,2,0:T(8,128)(2,1)} async-done(((bf16[16,512,1,256]{1,3,2,0:T(8,128)(2,1)}), bf16[16,512,1,256]{1,3,2,0:T(8,128)(2,1)}, u32[]{:S(2)}, u32[]{:S(2)}) %all-to-all-start.2) | async-done | bytes 4194336 | tf_op jit(solution)/shard_map/all_to_all | solution.py:107
  446.7 6.4 %copy.40 = bf16[16,512,1,256]{3,1,0,2:T(8,128)(2,1)} copy(bf16[16,512,1,256]{1,3,2,0:T(8,128)(2,1)} %all-to-all-done.2) | data formatting | bytes 8388608 | tf_op jit(solution)/shard_map/all_to_all | solution.py:107
  453.1 1.3 copy.62
  (48 shorter events, 18.5 us)
Async XLA Ops:
  7.2 161.4 %all-gather.3.cloned.1.call-start = ((), (), s32[]{:S(2)}) async-start(), calls=%async_computation.5 | async-start | bytes 17825792 | tf_op jit(solution)/shard_map/all_gather | solution.py:86
  7.9 213.3 %reduce-scatter.3.cloned.1.call-start = ((), (), s32[]{:S(2)}) async-start(), calls=%async_computation.6 | async-start | bytes 2359296 | tf_op jit(solution)/shard_map/reduce_scatter | solution.py:22
  177.6 43.7 %copy-start = (f32[512,128]{1,0:T(8,128)S(1)}, f32[512,128]{1,0:T(8,128)}, u32[]{:S(2)}) copy-start(f32[512,128]{1,0:T(8,128)} %param.10) | copy-start | bytes 786436
  177.6 43.8 %copy-start.1 = (f32[512,128]{1,0:T(8,128)S(1)}, f32[512,128]{1,0:T(8,128)}, u32[]{:S(2)}) copy-start(f32[512,128]{1,0:T(8,128)} %param.11) | copy-start | bytes 786436
  177.6 43.9 %copy-start.2 = (f32[512,128]{1,0:T(8,128)S(1)}, f32[512,128]{1,0:T(8,128)}, u32[]{:S(2)}) copy-start(f32[512,128]{1,0:T(8,128)} %param.9) | copy-start | bytes 786436
  180.1 59.6 %reduce-scatter.5.cloned.1.call-start = ((), (), s32[]{:S(2)}) async-start(), calls=%async_computation.7 | async-start | bytes 393216 | tf_op jit(solution)/shard_map/reduce_scatter | solution.py:22
  221.2 84.0 %all-gather.5.cloned.1.call-start = ((), (), s32[]{:S(2)}) async-start(), calls=%async_computation.8 | async-start | bytes 2228224 | tf_op jit(solution)/shard_map/all_gather | solution.py:95
  244.5 95.1 %all-to-all-start.1 = ((bf16[16,512,128]{2,1,0:T(8,128)(2,1)}), bf16[16,512,128]{2,1,0:T(8,128)(2,1)S(1)}, u32[]{:S(2)}, u32[]{:S(2)}) async-start(bf16[16,512,128]{2,1,0:T(8,128)(2,1)} %broadcast_in_dim.78), calls=%async_computation.3 | async-start | bytes 4194304 | tf_op jit(solution)/shard_map/all_to_all | solution.py:38
  339.6 107.1 %all-to-all-start.2 = ((bf16[16,512,1,256]{1,3,2,0:T(8,128)(2,1)}), bf16[16,512,1,256]{1,3,2,0:T(8,128)(2,1)}, u32[]{:S(2)}, u32[]{:S(2)}) async-start(bf16[16,512,1,256]{1,3,2,0:T(8,128)(2,1)} %fusion.2), calls=%async_computation.4 | async-start | bytes 8388608 | tf_op jit(solution)/shard_map/all_to_all | solution.py:107
Sparse Core Ops, SparseCore 0:
  10.5 158.0 all-gather.2
  180.3 40.8 reduce-scatter.2
  223.7 16.0 reduce-scatter.4
  242.8 62.2 all-gather.4
